TPU v7x, 32 devices: a whole 2x2x4 slice. The times are simulated.
32 devices in a mesh: group: 2 (over core), trow: 2 (over y), tcol: 8 (over z, x).
Axes of the slice: x: 2, y: 2, z: 4, core: 2. Of those that a mesh axis runs over, the one named last changes fastest.
Arguments:
- displacement: float32 [3, 128, 64, 256], P(None, ('group', 'trow'), 'tcol'), may hold values from -6 to 6
- velocity: float32 [3, 128, 64, 256], P(None, ('group', 'trow'), 'tcol'), may hold values from -6 to 6
- stiffness: float32 [128, 64], P(('group', 'trow'), 'tcol'), may hold values from 4 to 12
- wet_position: float32 [3, 8192], P(None, ('group', 'trow', 'tcol')), may hold values from -6 to 6
- wet_normal: float32 [3, 8192], P(None, ('group', 'trow', 'tcol')), may hold values from -6 to 6
- wet_area: float32 [8192], P(('group', 'trow', 'tcol')), may hold values from 0.022097087 to 0.22097087
- wet_map: int32 [8192], P(('group', 'trow', 'tcol')), may hold values from 0 to 255
Outputs:
- displacement_out: float32 [3, 128, 64, 256], P(None, ('group', 'trow'), 'tcol')
- velocity_out: float32 [3, 128, 64, 256], P(None, ('group', 'trow'), 'tcol')
Inputs may be any that keep to these rules, and one draw needn't show every extreme that they name: Each wet point lies on the patch of nodes of the device that holds it: wet_map gives a * 8 + b for the node (a, b) of that patch.
All inputs are finite; a program needn't handle non-finite values.
Results may differ from a plain program's by a relative error of at most 0.0018.
Values may be sent and summed in bfloat16 or wider, within the bound.
A program may use at most 128 MiB of HBM per device.

v0:
```python
import math
import jax
import jax.numpy as jnp
from jax import lax
from jax.sharding import PartitionSpec as P

LOADS = 64
SUBSTEPS = 4
COUPLED = 2
WET_DEV = 256
SPHERE_AREA = 4.0 * math.pi
SMOOTHING = 0.1
TIME_STEP = 0.3
THICKNESS = 0.5
SPLINE_TAPS = (2.0 / 3.0, -1.0 / 12.0, -1.0 / 12.0, -1.0 / 6.0)


def padded_2(array, sides, width):
    for axis, dim in sides:
        count, length = (lax.axis_size(axis), array.shape[dim])
        up = [(i, (i + 1) % count) for i in range(count - 1)]
        down = [(j, i) for i, j in up]
        last = lax.slice_in_dim(array, length - width, length, axis=dim)
        first = lax.slice_in_dim(array, 0, width, axis=dim)
        before = lax.ppermute(last, axis, up)
        after = lax.ppermute(first, axis, down)
        array = jnp.concatenate([before, array, after], axis=dim)
    return array


def spline_apply(padded, height, breadth, margin):
    middle = padded[:, margin : margin + height, margin : margin + breadth]
    summed = 2.0 * SPLINE_TAPS[0] * middle
    for offset in (1, 2, 3):
        along_rows = (
            padded[:, margin + offset : margin + offset + height, margin : margin + breadth]
            + padded[:, margin - offset : margin - offset + height, margin : margin + breadth]
        )
        along_cols = (
            padded[:, margin : margin + height, margin + offset : margin + offset + breadth]
            + padded[:, margin : margin + height, margin - offset : margin - offset + breadth]
        )
        summed = summed + SPLINE_TAPS[offset] * (along_rows + along_cols)
    return summed


def thickness_term(values, stride):
    above_layer = jnp.concatenate([values[..., stride:], values[..., -stride:]], axis=3)
    below_layer = jnp.concatenate([values[..., :stride], values[..., :-stride]], axis=3)
    return 2.0 * values - above_layer - below_layer


def advance(displacement, velocity, stiffness_grid, loading, in_plane):
    acceleration = -(stiffness_grid * in_plane) - THICKNESS * thickness_term(displacement, LOADS)
    outermost = acceleration[..., -LOADS:] + loading
    acceleration = jnp.concatenate([acceleration[..., :-LOADS], outermost], axis=3)
    velocity = velocity + TIME_STEP * acceleration
    displacement = displacement + TIME_STEP * velocity
    return (displacement, velocity)


def kernel_tile(position, normal, area, targets):
    delta_x = targets[0][None, :] - position[0][:, None]
    delta_y = targets[1][None, :] - position[1][:, None]
    delta_z = targets[2][None, :] - position[2][:, None]
    numerator = (
        normal[0][:, None] * delta_x + normal[1][:, None] * delta_y + normal[2][:, None] * delta_z
    )
    squared = delta_x * delta_x + delta_y * delta_y + delta_z * delta_z + SMOOTHING * SMOOTHING
    weighted = area[:, None] * numerator
    return (weighted / (SPHERE_AREA * squared * jnp.sqrt(squared))).astype(jnp.bfloat16)


def normal_speeds(velocity, wet_normal, wet_map):
    outer_layer = velocity[..., -LOADS:]
    flattened = outer_layer.reshape(3, outer_layer.shape[1] * outer_layer.shape[2], LOADS)
    picked = jnp.take(flattened, wet_map, axis=1)
    speeds = (
        wet_normal[0][:, None] * picked[0]
        + wet_normal[1][:, None] * picked[1]
        + wet_normal[2][:, None] * picked[2]
    )
    return speeds.T


def node_loads(pressure, wet_normal, wet_map, height, breadth):
    node_count = height * breadth
    one_hot = (
        lax.broadcasted_iota(jnp.int32, (node_count, wet_map.shape[0]), 0) == wet_map[None, :]
    ).astype(jnp.float32)
    contribution = -(wet_normal[:, None, :] * pressure[None, :, :])
    loading = jnp.einsum("pw,kqw->kpq", one_hot, contribution, precision=lax.Precision.HIGHEST)
    return loading.reshape(3, height, breadth, LOADS)


def pressure_terms(sources, targets, gathered, block_size, block_count):
    position, normal, area = sources

    def accumulate(block_index, summed):
        tile = kernel_tile(
            position,
            normal,
            area,
            lax.dynamic_slice_in_dim(targets, block_index * block_size, block_size, 1),
        )
        partial_value = jnp.dot(gathered, tile, preferred_element_type=jnp.float32)
        return lax.dynamic_update_slice_in_dim(summed, partial_value, block_index * block_size, 1)

    initial = jnp.zeros((gathered.shape[0], block_size * block_count), jnp.float32)
    return lax.fori_loop(0, block_count, accumulate, initial)


def on_device(displacement, velocity, stiffness, wet_position, wet_normal, wet_area, wet_map):
    height = displacement.shape[1]
    breadth = displacement.shape[2]
    targets = lax.all_gather(wet_position, ("group", "trow"), axis=1, tiled=True)
    sources = (
        lax.all_gather(wet_position, "tcol", axis=1, tiled=True),
        lax.all_gather(wet_normal, "tcol", axis=1, tiled=True),
        lax.all_gather(wet_area, "tcol", axis=0, tiled=True),
    )
    target_count = targets.shape[1]
    factor = 2
    block_size = WET_DEV * factor
    block_count = target_count // block_size
    stiffness_grid = stiffness[None, :, :, None]
    for repeat in range(COUPLED):
        speeds = normal_speeds(velocity, wet_normal, wet_map)
        speed_rounded = speeds.astype(jnp.bfloat16)
        gathered = lax.all_gather(speed_rounded, "tcol", axis=1, tiled=True)
        partial_value = pressure_terms(sources, targets, gathered, block_size, block_count)
        received = lax.psum_scatter(
            partial_value, ("group", "trow"), scatter_dimension=1, tiled=True
        )
        pressure = 0.5 * speeds + received
        loading = node_loads(pressure, wet_normal, wet_map, height, breadth)
        for substep in range(SUBSTEPS):
            padded = padded_2(displacement, ((("group", "trow"), 1), ("tcol", 2)), 3)
            in_plane = spline_apply(padded, height, breadth, 3)
            displacement, velocity = advance(
                displacement, velocity, stiffness_grid, loading, in_plane
            )
    return (displacement, velocity)


def solution(mesh):
    placed = (
        P(None, ("group", "trow"), "tcol", None),
        P(None, ("group", "trow"), "tcol", None),
        P(("group", "trow"), "tcol"),
        P(None, ("group", "trow", "tcol")),
        P(None, ("group", "trow", "tcol")),
        P(("group", "trow", "tcol")),
        P(("group", "trow", "tcol")),
    )
    return jax.shard_map(
        on_device,
        mesh=mesh,
        in_specs=placed,
        out_specs=(
            P(None, ("group", "trow"), "tcol", None),
            P(None, ("group", "trow"), "tcol", None),
        ),
        check_vma=False,
    )
```

profile of v0, /device:TPU:0, one launch (start us, length us, event | category | flops | bytes accessed | tf_op | source)
XLA Modules:
  0.0 489.0 jit_solution(4813544611088728946)
XLA Ops:
  8.1 4.9 %collective-permute-start.1 = (f32[3,3,8,256]{3,2,1,0:T(8,128)S(1)}, f32[3,3,8,256]{3,2,1,0:T(8,128)S(1)}, u32[]{:S(2)}, u32[]{:S(2)}) collective-permute-start(f32[3,3,8,256]{3,2,1,0:T(8,128)S(1)} %get-tuple-element.425), channel_id=1, source_target_pairs={{0,8},{8,16},{16,24},{1,9},{9,17},{17,25},{2,10},{10,18},{18,26},{... | collective-permute-start | bytes 221192 | tf_op jit(solution)/shard_map/ppermute | solution.py:25
  16.6 31.1 %all_gather.19 = f32[3,2048]{1,0:T(4,128)S(1)} all-gather(f32[3,256]{1,0:T(4,128)} %param.17), channel_id=1, replica_groups=mesh['group'=2,'trow'=2,'tcol'=8] {'tcol'}, dimensions={1}, use_global_device_ids=true | all-gather | bytes 27648 | tf_op jit(solution)/shard_map/all_gather | solution.py:119
  47.6 30.7 %all_gather.21 = f32[3,2048]{1,0:T(4,128)S(1)} all-gather(f32[3,256]{1,0:T(4,128)} %param.16), channel_id=1, replica_groups=mesh['group'=2,'trow'=2,'tcol'=8] {'tcol'}, dimensions={1}, use_global_device_ids=true | all-gather | bytes 27648 | tf_op jit(solution)/shard_map/all_gather | solution.py:118
  78.4 12.3 %all_gather.20 = f32[3,1024]{1,0:T(4,128)} all-gather(f32[3,256]{1,0:T(4,128)} %param.16), channel_id=1, replica_groups=mesh['group'=2,'trow'=2,'tcol'=8] {'group','trow'}, dimensions={1}, use_global_device_ids=true | all-gather | bytes 15360 | tf_op jit(solution)/shard_map/all_gather | solution.py:116
  94.0 31.3 %all_gather.22 = bf16[64,2048]{0,1:T(8,128)(2,1)S(1)} all-gather(bf16[64,256]{0,1:T(8,128)(2,1)S(1)} %get-tuple-element.319), channel_id=1, replica_groups=mesh['group'=2,'trow'=2,'tcol'=8] {'tcol'}, dimensions={1}, use_global_device_ids=true | all-gather | bytes 294912 | tf_op jit(solution)/shard_map/all_gather | solution.py:130
  125.4 20.6 %all-gather = f32[8,1,256]{2,1,0:T(1,128)S(1)} all-gather(f32[1,1,256]{2,1,0:T(1,128)S(1)} %bitcast.189), channel_id=1, replica_groups=mesh['group'=2,'trow'=2,'tcol'=8] {'tcol'}, dimensions={0}, use_global_device_ids=true | all-gather | bytes 9216 | tf_op jit(solution)/shard_map/all_gather | solution.py:120
  146.1 11.3 %while.26 = (s32[]{:T(128)}, f32[64,1024]{1,0:T(8,128)S(1)}, f32[2048]{0:T(1024)S(1)}, f32[3,2048]{1,0:T(4,128)S(1)}, f32[3,1024]{1,0:T(4,128)}, /*index=5*/f32[...) while((s32[]{:T(128)}, f32[64,1024]{1,0:T(8,128)S(1)}, ...), condition=%wide.region_1.3_spmd, body=%wide.region_0.0_spmd.sunk | while | flops 154140672 | bytes 567507 | solution.py:110
  162.3 5.4 %collective-permute-start.3 = (f32[3,38,3,256]{3,2,1,0:T(4,128)}, f32[3,38,3,256]{3,2,1,0:T(4,128)}, u32[]{:S(2)}, u32[]{:S(2)}) collective-permute-start(f32[3,38,3,256]{3,2,1,0:T(4,128)} %get-tuple-element.374), channel_id=1, source_target_pairs={{0,1},{1,2},{2,3},{3,4},{4,5},{5,6},{6,7},{8,9},{9,10},{10,11},{11... | collective-permute-start | bytes 1050632 | tf_op jit(solution)/shard_map/ppermute | solution.py:25
  173.2 5.7 %fusion.156 = f32[3,32,8,256]{3,2,1,0:T(8,128)S(1)} fusion(f32[3,38,8,256]{3,2,1,0:T(8,128)} %copy-done.5, f32[3,38,3,256]{3,2,1,0:T(4,128)} %collective-permute-done.3, f32[3,38,3,256]{3,2,1,0:T(4,128)} %copy-done.16, f32[3,35,8,256]{3,2,1,0:T(8,128)} %copy-done.3, f32[3,35,8,256]{3,2,1,0:T(8,128)S(1)} %get-tuple-element.429, ...), kind=kLoop, calls=%fused_computation.249 | loop fusion | flops 6094848 | bytes 9499648 | tf_op jit(solution)/shard_map/sub | solution.py:54
  190.4 5.2 %collective-permute-start.7 = (f32[3,38,3,256]{3,2,1,0:T(4,128)S(1)}, f32[3,38,3,256]{3,2,1,0:T(4,128)S(1)}, u32[]{:S(2)}, u32[]{:S(2)}) collective-permute-start(f32[3,38,3,256]{3,2,1,0:T(4,128)S(1)} %get-tuple-element.372), channel_id=1, source_target_pairs={{0,1},{1,2},{2,3},{3,4},{4,5},{5,6},{6,7},{8,9},{9,10},{10,11},{11... | collective-permute-start | bytes 1050632 | tf_op jit(solution)/shard_map/ppermute | solution.py:25
  196.1 8.9 %collective-permute-done.6 = f32[3,38,3,256]{3,2,1,0:T(4,128)S(1)} collective-permute-done((f32[3,38,3,256]{3,2,1,0:T(4,128)S(1)}, f32[3,38,3,256]{3,2,1,0:T(4,128)S(1)}, u32[]{:S(2)}, u32[]{:S(2)}) %collective-permute-start.6) | collective-permute-done | bytes 350240 | tf_op jit(solution)/shard_map/ppermute | solution.py:26
  204.9 10.2 %collective-permute-done.7 = f32[3,38,3,256]{3,2,1,0:T(4,128)S(1)} collective-permute-done((f32[3,38,3,256]{3,2,1,0:T(4,128)S(1)}, f32[3,38,3,256]{3,2,1,0:T(4,128)S(1)}, u32[]{:S(2)}, u32[]{:S(2)}) %collective-permute-start.7) | collective-permute-done | bytes 350240 | tf_op jit(solution)/shard_map/ppermute | solution.py:25
  227.2 5.0 %collective-permute-start.11 = (f32[3,38,3,256]{3,2,1,0:T(4,128)S(1)}, f32[3,38,3,256]{3,2,1,0:T(4,128)S(1)}, u32[]{:S(2)}, u32[]{:S(2)}) collective-permute-start(f32[3,38,3,256]{3,2,1,0:T(4,128)S(1)} %get-tuple-element.368), channel_id=1, source_target_pairs={{0,1},{1,2},{2,3},{3,4},{4,5},{5,6},{6,7},{8,9},{9,10},{10,11},{11... | collective-permute-start | bytes 1050632 | tf_op jit(solution)/shard_map/ppermute | solution.py:25
  232.7 8.6 %collective-permute-done.10 = f32[3,38,3,256]{3,2,1,0:T(4,128)S(1)} collective-permute-done((f32[3,38,3,256]{3,2,1,0:T(4,128)S(1)}, f32[3,38,3,256]{3,2,1,0:T(4,128)S(1)}, u32[]{:S(2)}, u32[]{:S(2)}) %collective-permute-start.10) | collective-permute-done | bytes 350240 | tf_op jit(solution)/shard_map/ppermute | solution.py:26
  241.3 10.2 %collective-permute-done.11 = f32[3,38,3,256]{3,2,1,0:T(4,128)S(1)} collective-permute-done((f32[3,38,3,256]{3,2,1,0:T(4,128)S(1)}, f32[3,38,3,256]{3,2,1,0:T(4,128)S(1)}, u32[]{:S(2)}, u32[]{:S(2)}) %collective-permute-start.11) | collective-permute-done | bytes 350240 | tf_op jit(solution)/shard_map/ppermute | solution.py:25
  263.8 5.0 %collective-permute-start.15 = (f32[3,38,3,256]{3,2,1,0:T(4,128)S(1)}, f32[3,38,3,256]{3,2,1,0:T(4,128)S(1)}, u32[]{:S(2)}, u32[]{:S(2)}) collective-permute-start(f32[3,38,3,256]{3,2,1,0:T(4,128)S(1)} %get-tuple-element.364), channel_id=1, source_target_pairs={{0,1},{1,2},{2,3},{3,4},{4,5},{5,6},{6,7},{8,9},{9,10},{10,11},{11... | collective-permute-start | bytes 1050632 | tf_op jit(solution)/shard_map/ppermute | solution.py:25
  269.3 9.1 %collective-permute-done.14 = f32[3,38,3,256]{3,2,1,0:T(4,128)S(1)} collective-permute-done((f32[3,38,3,256]{3,2,1,0:T(4,128)S(1)}, f32[3,38,3,256]{3,2,1,0:T(4,128)S(1)}, u32[]{:S(2)}, u32[]{:S(2)}) %collective-permute-start.14) | collective-permute-done | bytes 350240 | tf_op jit(solution)/shard_map/ppermute | solution.py:26
  278.4 10.3 %collective-permute-done.15 = f32[3,38,3,256]{3,2,1,0:T(4,128)S(1)} collective-permute-done((f32[3,38,3,256]{3,2,1,0:T(4,128)S(1)}, f32[3,38,3,256]{3,2,1,0:T(4,128)S(1)}, u32[]{:S(2)}, u32[]{:S(2)}) %collective-permute-start.15) | collective-permute-done | bytes 350240 | tf_op jit(solution)/shard_map/ppermute | solution.py:25
  293.9 31.5 %all_gather.23 = bf16[64,2048]{0,1:T(8,128)(2,1)S(1)} all-gather(bf16[64,256]{0,1:T(8,128)(2,1)S(1)} %get-tuple-element.313), channel_id=1, replica_groups=mesh['group'=2,'trow'=2,'tcol'=8] {'tcol'}, dimensions={1}, use_global_device_ids=true | all-gather | bytes 294912 | tf_op jit(solution)/shard_map/all_gather | solution.py:130
  327.0 4.8 collective-permute-start.17
  331.8 11.3 %while.27 = (s32[]{:T(128)}, f32[64,1024]{1,0:T(8,128)S(1)}, f32[2048]{0:T(1024)S(1)}, f32[3,2048]{1,0:T(4,128)S(1)}, f32[3,1024]{1,0:T(4,128)}, /*index=5*/f32[...) while((s32[]{:T(128)}, f32[64,1024]{1,0:T(8,128)S(1)}, ...), condition=%wide.region_4.6_spmd, body=%wide.region_3.5_spmd.sunk | while | flops 154140672 | bytes 567507 | solution.py:110
  345.4 5.3 %collective-permute-start.19 = (f32[3,38,3,256]{3,2,1,0:T(4,128)S(1)}, f32[3,38,3,256]{3,2,1,0:T(4,128)}, u32[]{:S(2)}, u32[]{:S(2)}) collective-permute-start(f32[3,38,3,256]{3,2,1,0:T(4,128)S(1)} %get-tuple-element.360), channel_id=1, source_target_pairs={{0,1},{1,2},{2,3},{3,4},{4,5},{5,6},{6,7},{8,9},{9,10},{10,11},{11... | collective-permute-start | bytes 1050632 | tf_op jit(solution)/shard_map/ppermute | solution.py:25
  352.2 4.9 collective-permute-done.18
  357.1 8.0 %collective-permute-done.19 = f32[3,38,3,256]{3,2,1,0:T(4,128)} collective-permute-done((f32[3,38,3,256]{3,2,1,0:T(4,128)S(1)}, f32[3,38,3,256]{3,2,1,0:T(4,128)}, u32[]{:S(2)}, u32[]{:S(2)}) %collective-permute-start.19) | collective-permute-done | bytes 350240 | tf_op jit(solution)/shard_map/ppermute | solution.py:25
  386.5 8.5 %collective-permute-done.22 = f32[3,38,3,256]{3,2,1,0:T(4,128)S(1)} collective-permute-done((f32[3,38,3,256]{3,2,1,0:T(4,128)S(1)}, f32[3,38,3,256]{3,2,1,0:T(4,128)S(1)}, u32[]{:S(2)}, u32[]{:S(2)}) %collective-permute-start.22) | collective-permute-done | bytes 350240 | tf_op jit(solution)/shard_map/ppermute | solution.py:26
  395.0 10.2 %collective-permute-done.23 = f32[3,38,3,256]{3,2,1,0:T(4,128)S(1)} collective-permute-done((f32[3,38,3,256]{3,2,1,0:T(4,128)S(1)}, f32[3,38,3,256]{3,2,1,0:T(4,128)S(1)}, u32[]{:S(2)}, u32[]{:S(2)}) %collective-permute-start.23) | collective-permute-done | bytes 350240 | tf_op jit(solution)/shard_map/ppermute | solution.py:25
  417.2 5.3 %collective-permute-start.27 = (f32[3,38,3,256]{3,2,1,0:T(4,128)S(1)}, f32[3,38,3,256]{3,2,1,0:T(4,128)S(1)}, u32[]{:S(2)}, u32[]{:S(2)}) collective-permute-start(f32[3,38,3,256]{3,2,1,0:T(4,128)S(1)} %get-tuple-element.352), channel_id=1, source_target_pairs={{0,1},{1,2},{2,3},{3,4},{4,5},{5,6},{6,7},{8,9},{9,10},{10,11},{11... | collective-permute-start | bytes 1050632 | tf_op jit(solution)/shard_map/ppermute | solution.py:25
  423.0 8.8 %collective-permute-done.26 = f32[3,38,3,256]{3,2,1,0:T(4,128)S(1)} collective-permute-done((f32[3,38,3,256]{3,2,1,0:T(4,128)S(1)}, f32[3,38,3,256]{3,2,1,0:T(4,128)S(1)}, u32[]{:S(2)}, u32[]{:S(2)}) %collective-permute-start.26) | collective-permute-done | bytes 350240 | tf_op jit(solution)/shard_map/ppermute | solution.py:26
  431.8 10.2 %collective-permute-done.27 = f32[3,38,3,256]{3,2,1,0:T(4,128)S(1)} collective-permute-done((f32[3,38,3,256]{3,2,1,0:T(4,128)S(1)}, f32[3,38,3,256]{3,2,1,0:T(4,128)S(1)}, u32[]{:S(2)}, u32[]{:S(2)}) %collective-permute-start.27) | collective-permute-done | bytes 350240 | tf_op jit(solution)/shard_map/ppermute | solution.py:25
  454.0 5.0 %collective-permute-start.31 = (f32[3,38,3,256]{3,2,1,0:T(4,128)S(1)}, f32[3,38,3,256]{3,2,1,0:T(4,128)S(1)}, u32[]{:S(2)}, u32[]{:S(2)}) collective-permute-start(f32[3,38,3,256]{3,2,1,0:T(4,128)S(1)} %get-tuple-element.348), channel_id=1, source_target_pairs={{0,1},{1,2},{2,3},{3,4},{4,5},{5,6},{6,7},{8,9},{9,10},{10,11},{11... | collective-permute-start | bytes 1050632 | tf_op jit(solution)/shard_map/ppermute | solution.py:25
  459.5 8.6 %collective-permute-done.30 = f32[3,38,3,256]{3,2,1,0:T(4,128)S(1)} collective-permute-done((f32[3,38,3,256]{3,2,1,0:T(4,128)S(1)}, f32[3,38,3,256]{3,2,1,0:T(4,128)S(1)}, u32[]{:S(2)}, u32[]{:S(2)}) %collective-permute-start.30) | collective-permute-done | bytes 350240 | tf_op jit(solution)/shard_map/ppermute | solution.py:26
  468.1 10.2 %collective-permute-done.31 = f32[3,38,3,256]{3,2,1,0:T(4,128)S(1)} collective-permute-done((f32[3,38,3,256]{3,2,1,0:T(4,128)S(1)}, f32[3,38,3,256]{3,2,1,0:T(4,128)S(1)}, u32[]{:S(2)}, u32[]{:S(2)}) %collective-permute-start.31) | collective-permute-done | bytes 350240 | tf_op jit(solution)/shard_map/ppermute | solution.py:25
  (229 shorter events, 137.9 us)
Async XLA Ops:
  7.2 171.8 %reduce-scatter.3.cloned.1.call-start = ((), (), s32[]{:S(2)}) async-start(), calls=%async_computation.2 | async-start | bytes 655360 | tf_op jit(solution)/shard_map/reduce_scatter | solution.py:132
  8.1 150.4 %collective-permute-start.1 = (f32[3,3,8,256]{3,2,1,0:T(8,128)S(1)}, f32[3,3,8,256]{3,2,1,0:T(8,128)S(1)}, u32[]{:S(2)}, u32[]{:S(2)}) collective-permute-start(f32[3,3,8,256]{3,2,1,0:T(8,128)S(1)} %get-tuple-element.425), channel_id=1, source_target_pairs={{0,8},{8,16},{16,24},{1,9},{9,17},{17,25},{2,10},{10,18},{18,26},{... | collective-permute-start | bytes 221192 | tf_op jit(solution)/shard_map/ppermute | solution.py:25
  13.1 145.8 %collective-permute-start = (f32[3,3,8,256]{3,2,1,0:T(8,128)S(1)}, f32[3,3,8,256]{3,2,1,0:T(8,128)S(1)}, u32[]{:S(2)}, u32[]{:S(2)}) collective-permute-start(f32[3,3,8,256]{3,2,1,0:T(8,128)S(1)} %get-tuple-element.424), channel_id=1, source_target_pairs={{8,0},{16,8},{24,16},{9,1},{17,9},{25,17},{10,2},{18,10},{26,18},{... | collective-permute-start | bytes 221192 | tf_op jit(solution)/shard_map/ppermute | solution.py:26
  158.5 211.7 %reduce-scatter.5.cloned.1.call-start = ((), (), s32[]{:S(2)}) async-start(), calls=%async_computation.3 | async-start | bytes 655360 | tf_op jit(solution)/shard_map/reduce_scatter | solution.py:132
  161.0 10.7 %collective-permute-start.2 = (f32[3,38,3,256]{3,2,1,0:T(4,128)}, f32[3,38,3,256]{3,2,1,0:T(4,128)S(1)}, u32[]{:S(2)}, u32[]{:S(2)}) collective-permute-start(f32[3,38,3,256]{3,2,1,0:T(4,128)} %get-tuple-element.373), channel_id=1, source_target_pairs={{1,0},{2,1},{3,2},{4,3},{5,4},{6,5},{7,6},{9,8},{10,9},{11,10},{12... | collective-permute-start | bytes 1050632 | tf_op jit(solution)/shard_map/ppermute | solution.py:26
  162.3 10.9 %collective-permute-start.3 = (f32[3,38,3,256]{3,2,1,0:T(4,128)}, f32[3,38,3,256]{3,2,1,0:T(4,128)}, u32[]{:S(2)}, u32[]{:S(2)}) collective-permute-start(f32[3,38,3,256]{3,2,1,0:T(4,128)} %get-tuple-element.374), channel_id=1, source_target_pairs={{0,1},{1,2},{2,3},{3,4},{4,5},{5,6},{6,7},{8,9},{9,10},{10,11},{11... | collective-permute-start | bytes 1050632 | tf_op jit(solution)/shard_map/ppermute | solution.py:25
  181.0 6.2 %collective-permute-start.4 = (f32[3,3,8,256]{3,2,1,0:T(8,128)S(1)}, f32[3,3,8,256]{3,2,1,0:T(8,128)S(1)}, u32[]{:S(2)}, u32[]{:S(2)}) collective-permute-start(f32[3,3,8,256]{3,2,1,0:T(8,128)S(1)} %get-tuple-element.415), channel_id=1, source_target_pairs={{8,0},{16,8},{24,16},{9,1},{17,9},{25,17},{10,2},{18,10},{26,18},{... | collective-permute-start | bytes 221192 | tf_op jit(solution)/shard_map/ppermute | solution.py:26
  182.3 6.5 %collective-permute-start.5 = (f32[3,3,8,256]{3,2,1,0:T(8,128)S(1)}, f32[3,3,8,256]{3,2,1,0:T(8,128)S(1)}, u32[]{:S(2)}, u32[]{:S(2)}) collective-permute-start(f32[3,3,8,256]{3,2,1,0:T(8,128)S(1)} %get-tuple-element.416), channel_id=1, source_target_pairs={{0,8},{8,16},{16,24},{1,9},{9,17},{17,25},{2,10},{10,18},{18,26},{... | collective-permute-start | bytes 221192 | tf_op jit(solution)/shard_map/ppermute | solution.py:25
  189.1 15.8 %collective-permute-start.6 = (f32[3,38,3,256]{3,2,1,0:T(4,128)S(1)}, f32[3,38,3,256]{3,2,1,0:T(4,128)S(1)}, u32[]{:S(2)}, u32[]{:S(2)}) collective-permute-start(f32[3,38,3,256]{3,2,1,0:T(4,128)S(1)} %get-tuple-element.371), channel_id=1, source_target_pairs={{1,0},{2,1},{3,2},{4,3},{5,4},{6,5},{7,6},{9,8},{10,9},{11,10},{12... | collective-permute-start | bytes 1050632 | tf_op jit(solution)/shard_map/ppermute | solution.py:26
  190.4 24.7 %collective-permute-start.7 = (f32[3,38,3,256]{3,2,1,0:T(4,128)S(1)}, f32[3,38,3,256]{3,2,1,0:T(4,128)S(1)}, u32[]{:S(2)}, u32[]{:S(2)}) collective-permute-start(f32[3,38,3,256]{3,2,1,0:T(4,128)S(1)} %get-tuple-element.372), channel_id=1, source_target_pairs={{0,1},{1,2},{2,3},{3,4},{4,5},{5,6},{6,7},{8,9},{9,10},{10,11},{11... | collective-permute-start | bytes 1050632 | tf_op jit(solution)/shard_map/ppermute | solution.py:25
  217.9 6.2 %collective-permute-start.8 = (f32[3,3,8,256]{3,2,1,0:T(8,128)S(1)}, f32[3,3,8,256]{3,2,1,0:T(8,128)S(1)}, u32[]{:S(2)}, u32[]{:S(2)}) collective-permute-start(f32[3,3,8,256]{3,2,1,0:T(8,128)S(1)} %get-tuple-element.409), channel_id=1, source_target_pairs={{8,0},{16,8},{24,16},{9,1},{17,9},{25,17},{10,2},{18,10},{26,18},{... | collective-permute-start | bytes 221192 | tf_op jit(solution)/shard_map/ppermute | solution.py:26
  219.2 6.5 %collective-permute-start.9 = (f32[3,3,8,256]{3,2,1,0:T(8,128)S(1)}, f32[3,3,8,256]{3,2,1,0:T(8,128)S(1)}, u32[]{:S(2)}, u32[]{:S(2)}) collective-permute-start(f32[3,3,8,256]{3,2,1,0:T(8,128)S(1)} %get-tuple-element.410), channel_id=1, source_target_pairs={{0,8},{8,16},{16,24},{1,9},{9,17},{17,25},{2,10},{10,18},{18,26},{... | collective-permute-start | bytes 221192 | tf_op jit(solution)/shard_map/ppermute | solution.py:25
  225.9 15.4 %collective-permute-start.10 = (f32[3,38,3,256]{3,2,1,0:T(4,128)S(1)}, f32[3,38,3,256]{3,2,1,0:T(4,128)S(1)}, u32[]{:S(2)}, u32[]{:S(2)}) collective-permute-start(f32[3,38,3,256]{3,2,1,0:T(4,128)S(1)} %get-tuple-element.367), channel_id=1, source_target_pairs={{1,0},{2,1},{3,2},{4,3},{5,4},{6,5},{7,6},{9,8},{10,9},{11,10},{12... | collective-permute-start | bytes 1050632 | tf_op jit(solution)/shard_map/ppermute | solution.py:26
  227.2 24.3 %collective-permute-start.11 = (f32[3,38,3,256]{3,2,1,0:T(4,128)S(1)}, f32[3,38,3,256]{3,2,1,0:T(4,128)S(1)}, u32[]{:S(2)}, u32[]{:S(2)}) collective-permute-start(f32[3,38,3,256]{3,2,1,0:T(4,128)S(1)} %get-tuple-element.368), channel_id=1, source_target_pairs={{0,1},{1,2},{2,3},{3,4},{4,5},{5,6},{6,7},{8,9},{9,10},{10,11},{11... | collective-permute-start | bytes 1050632 | tf_op jit(solution)/shard_map/ppermute | solution.py:25
  254.1 6.2 %collective-permute-start.12 = (f32[3,3,8,256]{3,2,1,0:T(8,128)S(1)}, f32[3,3,8,256]{3,2,1,0:T(8,128)S(1)}, u32[]{:S(2)}, u32[]{:S(2)}) collective-permute-start(f32[3,3,8,256]{3,2,1,0:T(8,128)S(1)} %get-tuple-element.403), channel_id=1, source_target_pairs={{8,0},{16,8},{24,16},{9,1},{17,9},{25,17},{10,2},{18,10},{26,18},{... | collective-permute-start | bytes 221192 | tf_op jit(solution)/shard_map/ppermute | solution.py:26
  255.4 6.5 %collective-permute-start.13 = (f32[3,3,8,256]{3,2,1,0:T(8,128)S(1)}, f32[3,3,8,256]{3,2,1,0:T(8,128)S(1)}, u32[]{:S(2)}, u32[]{:S(2)}) collective-permute-start(f32[3,3,8,256]{3,2,1,0:T(8,128)S(1)} %get-tuple-element.404), channel_id=1, source_target_pairs={{0,8},{8,16},{16,24},{1,9},{9,17},{17,25},{2,10},{10,18},{18,26},{... | collective-permute-start | bytes 221192 | tf_op jit(solution)/shard_map/ppermute | solution.py:25
  262.5 15.9 %collective-permute-start.14 = (f32[3,38,3,256]{3,2,1,0:T(4,128)S(1)}, f32[3,38,3,256]{3,2,1,0:T(4,128)S(1)}, u32[]{:S(2)}, u32[]{:S(2)}) collective-permute-start(f32[3,38,3,256]{3,2,1,0:T(4,128)S(1)} %get-tuple-element.363), channel_id=1, source_target_pairs={{1,0},{2,1},{3,2},{4,3},{5,4},{6,5},{7,6},{9,8},{10,9},{11,10},{12... | collective-permute-start | bytes 1050632 | tf_op jit(solution)/shard_map/ppermute | solution.py:26
  263.8 24.8 %collective-permute-start.15 = (f32[3,38,3,256]{3,2,1,0:T(4,128)S(1)}, f32[3,38,3,256]{3,2,1,0:T(4,128)S(1)}, u32[]{:S(2)}, u32[]{:S(2)}) collective-permute-start(f32[3,38,3,256]{3,2,1,0:T(4,128)S(1)} %get-tuple-element.364), channel_id=1, source_target_pairs={{0,1},{1,2},{2,3},{3,4},{4,5},{5,6},{6,7},{8,9},{9,10},{10,11},{11... | collective-permute-start | bytes 1050632 | tf_op jit(solution)/shard_map/ppermute | solution.py:25
  325.7 17.5 %collective-permute-start.16 = (f32[3,3,8,256]{3,2,1,0:T(8,128)S(1)}, f32[3,3,8,256]{3,2,1,0:T(8,128)S(1)}, u32[]{:S(2)}, u32[]{:S(2)}) collective-permute-start(f32[3,3,8,256]{3,2,1,0:T(8,128)S(1)} %get-tuple-element.397), channel_id=1, source_target_pairs={{8,0},{16,8},{24,16},{9,1},{17,9},{25,17},{10,2},{18,10},{26,18},{... | collective-permute-start | bytes 221192 | tf_op jit(solution)/shard_map/ppermute | solution.py:26
  327.0 16.2 %collective-permute-start.17 = (f32[3,3,8,256]{3,2,1,0:T(8,128)S(1)}, f32[3,3,8,256]{3,2,1,0:T(8,128)S(1)}, u32[]{:S(2)}, u32[]{:S(2)}) collective-permute-start(f32[3,3,8,256]{3,2,1,0:T(8,128)S(1)} %get-tuple-element.398), channel_id=1, source_target_pairs={{0,8},{8,16},{16,24},{1,9},{9,17},{17,25},{2,10},{10,18},{18,26},{... | collective-permute-start | bytes 221192 | tf_op jit(solution)/shard_map/ppermute | solution.py:25
  344.1 13.0 %collective-permute-start.18 = (f32[3,38,3,256]{3,2,1,0:T(4,128)}, f32[3,38,3,256]{3,2,1,0:T(4,128)}, u32[]{:S(2)}, u32[]{:S(2)}) collective-permute-start(f32[3,38,3,256]{3,2,1,0:T(4,128)} %get-tuple-element.359), channel_id=1, source_target_pairs={{1,0},{2,1},{3,2},{4,3},{5,4},{6,5},{7,6},{9,8},{10,9},{11,10},{12... | collective-permute-start | bytes 1050632 | tf_op jit(solution)/shard_map/ppermute | solution.py:26
  345.4 19.7 %collective-permute-start.19 = (f32[3,38,3,256]{3,2,1,0:T(4,128)S(1)}, f32[3,38,3,256]{3,2,1,0:T(4,128)}, u32[]{:S(2)}, u32[]{:S(2)}) collective-permute-start(f32[3,38,3,256]{3,2,1,0:T(4,128)S(1)} %get-tuple-element.360), channel_id=1, source_target_pairs={{0,1},{1,2},{2,3},{3,4},{4,5},{5,6},{6,7},{8,9},{9,10},{10,11},{11... | collective-permute-start | bytes 1050632 | tf_op jit(solution)/shard_map/ppermute | solution.py:25
  372.1 6.2 %collective-permute-start.20 = (f32[3,3,8,256]{3,2,1,0:T(8,128)S(1)}, f32[3,3,8,256]{3,2,1,0:T(8,128)S(1)}, u32[]{:S(2)}, u32[]{:S(2)}) collective-permute-start(f32[3,3,8,256]{3,2,1,0:T(8,128)S(1)} %get-tuple-element.391), channel_id=1, source_target_pairs={{8,0},{16,8},{24,16},{9,1},{17,9},{25,17},{10,2},{18,10},{26,18},{... | collective-permute-start | bytes 221192 | tf_op jit(solution)/shard_map/ppermute | solution.py:26
  373.4 6.5 %collective-permute-start.21 = (f32[3,3,8,256]{3,2,1,0:T(8,128)S(1)}, f32[3,3,8,256]{3,2,1,0:T(8,128)S(1)}, u32[]{:S(2)}, u32[]{:S(2)}) collective-permute-start(f32[3,3,8,256]{3,2,1,0:T(8,128)S(1)} %get-tuple-element.392), channel_id=1, source_target_pairs={{0,8},{8,16},{16,24},{1,9},{9,17},{17,25},{2,10},{10,18},{18,26},{... | collective-permute-start | bytes 221192 | tf_op jit(solution)/shard_map/ppermute | solution.py:25
  380.2 14.8 %collective-permute-start.22 = (f32[3,38,3,256]{3,2,1,0:T(4,128)S(1)}, f32[3,38,3,256]{3,2,1,0:T(4,128)S(1)}, u32[]{:S(2)}, u32[]{:S(2)}) collective-permute-start(f32[3,38,3,256]{3,2,1,0:T(4,128)S(1)} %get-tuple-element.355), channel_id=1, source_target_pairs={{1,0},{2,1},{3,2},{4,3},{5,4},{6,5},{7,6},{9,8},{10,9},{11,10},{12... | collective-permute-start | bytes 1050632 | tf_op jit(solution)/shard_map/ppermute | solution.py:26
  381.5 23.7 %collective-permute-start.23 = (f32[3,38,3,256]{3,2,1,0:T(4,128)S(1)}, f32[3,38,3,256]{3,2,1,0:T(4,128)S(1)}, u32[]{:S(2)}, u32[]{:S(2)}) collective-permute-start(f32[3,38,3,256]{3,2,1,0:T(4,128)S(1)} %get-tuple-element.356), channel_id=1, source_target_pairs={{0,1},{1,2},{2,3},{3,4},{4,5},{5,6},{6,7},{8,9},{9,10},{10,11},{11... | collective-permute-start | bytes 1050632 | tf_op jit(solution)/shard_map/ppermute | solution.py:25
  409.2 6.5 %collective-permute-start.25 = (f32[3,3,8,256]{3,2,1,0:T(8,128)S(1)}, f32[3,3,8,256]{3,2,1,0:T(8,128)S(1)}, u32[]{:S(2)}, u32[]{:S(2)}) collective-permute-start(f32[3,3,8,256]{3,2,1,0:T(8,128)S(1)} %get-tuple-element.386), channel_id=1, source_target_pairs={{0,8},{8,16},{16,24},{1,9},{9,17},{17,25},{2,10},{10,18},{18,26},{... | collective-permute-start | bytes 221192 | tf_op jit(solution)/shard_map/ppermute | solution.py:25
  415.9 15.9 %collective-permute-start.26 = (f32[3,38,3,256]{3,2,1,0:T(4,128)S(1)}, f32[3,38,3,256]{3,2,1,0:T(4,128)S(1)}, u32[]{:S(2)}, u32[]{:S(2)}) collective-permute-start(f32[3,38,3,256]{3,2,1,0:T(4,128)S(1)} %get-tuple-element.351), channel_id=1, source_target_pairs={{1,0},{2,1},{3,2},{4,3},{5,4},{6,5},{7,6},{9,8},{10,9},{11,10},{12... | collective-permute-start | bytes 1050632 | tf_op jit(solution)/shard_map/ppermute | solution.py:26
  417.2 24.8 %collective-permute-start.27 = (f32[3,38,3,256]{3,2,1,0:T(4,128)S(1)}, f32[3,38,3,256]{3,2,1,0:T(4,128)S(1)}, u32[]{:S(2)}, u32[]{:S(2)}) collective-permute-start(f32[3,38,3,256]{3,2,1,0:T(4,128)S(1)} %get-tuple-element.352), channel_id=1, source_target_pairs={{0,1},{1,2},{2,3},{3,4},{4,5},{5,6},{6,7},{8,9},{9,10},{10,11},{11... | collective-permute-start | bytes 1050632 | tf_op jit(solution)/shard_map/ppermute | solution.py:25
  445.9 6.5 %collective-permute-start.29 = (f32[3,3,8,256]{3,2,1,0:T(8,128)S(1)}, f32[3,3,8,256]{3,2,1,0:T(8,128)S(1)}, u32[]{:S(2)}, u32[]{:S(2)}) collective-permute-start(f32[3,3,8,256]{3,2,1,0:T(8,128)S(1)} %get-tuple-element.380), channel_id=1, source_target_pairs={{0,8},{8,16},{16,24},{1,9},{9,17},{17,25},{2,10},{10,18},{18,26},{... | collective-permute-start | bytes 221192 | tf_op jit(solution)/shard_map/ppermute | solution.py:25
  452.7 15.4 %collective-permute-start.30 = (f32[3,38,3,256]{3,2,1,0:T(4,128)S(1)}, f32[3,38,3,256]{3,2,1,0:T(4,128)S(1)}, u32[]{:S(2)}, u32[]{:S(2)}) collective-permute-start(f32[3,38,3,256]{3,2,1,0:T(4,128)S(1)} %get-tuple-element.347), channel_id=1, source_target_pairs={{1,0},{2,1},{3,2},{4,3},{5,4},{6,5},{7,6},{9,8},{10,9},{11,10},{12... | collective-permute-start | bytes 1050632 | tf_op jit(solution)/shard_map/ppermute | solution.py:26
  454.0 24.3 %collective-permute-start.31 = (f32[3,38,3,256]{3,2,1,0:T(4,128)S(1)}, f32[3,38,3,256]{3,2,1,0:T(4,128)S(1)}, u32[]{:S(2)}, u32[]{:S(2)}) collective-permute-start(f32[3,38,3,256]{3,2,1,0:T(4,128)S(1)} %get-tuple-element.348), channel_id=1, source_target_pairs={{0,1},{1,2},{2,3},{3,4},{4,5},{5,6},{6,7},{8,9},{9,10},{10,11},{11... | collective-permute-start | bytes 1050632 | tf_op jit(solution)/shard_map/ppermute | solution.py:25
  (36 other events, 634.0 us)
Sparse Core Ops, SparseCore 0:
  158.6 18.0 reduce-scatter.2
  352.1 18.0 reduce-scatter.4
where the time goes:
time: 491 us; the launch traced here: 489 us
  blocking collectives  157 us (32%)
  waiting for transfers between devices  143 us (29%)
  starting transfers between devices  98.5 us (20%)
  other arithmetic  33 us (7%)
  local copies, waits for them, and re-layouts  22.1 us (5%)
  matrix products  19.5 us (4%)
  between operations  15.3 us (3%)
    ppermute x16, waiting for transfers between devices, padded_2(): before = lax.ppermute(last, axis, up)  80.1 us
    ppermute x16, starting transfers between devices, padded_2(): before = lax.ppermute(last, axis, up)  77.8 us
    all_gather x2, blocking collectives, on_device(): gathered = lax.all_gather(speed_rounded, 'tcol', axis=1, tiled=True)  62.8 us
    ppermute x16, waiting for transfers between devices, padded_2(): after = lax.ppermute(first, axis, down)  62.1 us
    all_gather x1, blocking collectives, on_device(): lax.all_gather(wet_normal, 'tcol', axis=1, tiled=True)  31.1 us
    all_gather x1, blocking collectives, on_device(): lax.all_gather(wet_position, 'tcol', axis=1, tiled=True)  30.7 us
    ppermute x16, starting transfers between devices, padded_2(): after = lax.ppermute(first, axis, down)  20.6 us
    all_gather x1, blocking collectives, on_device(): lax.all_gather(wet_area, 'tcol', axis=0, tiled=True)  20.6 us
  transfers between devices with their start and end apart: 34, of which 29 were waited for; matrix products, arithmetic and copies ran while one was open for 9% of the time, Pallas kernels for 0%

commit v1 on v0

--- a/solution.py
+++ b/solution.py
@@ -127,7 +127,7 @@
     for repeat in range(COUPLED):
         speeds = normal_speeds(velocity, wet_normal, wet_map)
         speed_rounded = speeds.astype(jnp.bfloat16)
-        gathered = lax.all_gather(speed_rounded, "tcol", axis=1, tiled=True)
+        gathered = jnp.concatenate(lax.all_gather(speed_rounded, "tcol"), axis=1)
         partial_value = pressure_terms(sources, targets, gathered, block_size, block_count)
         received = lax.psum_scatter(
             partial_value, ("group", "trow"), scatter_dimension=1, tiled=True

time: 491 us -> 490 us (level)
  no operation moved by 1% of the time
where the time goes in v1:
time: 490 us; the launch traced here: 488 us
  blocking collectives  156 us (32%)
  waiting for transfers between devices  143 us (29%)
  starting transfers between devices  98.8 us (20%)
  other arithmetic  33 us (7%)
  local copies, waits for them, and re-layouts  22.1 us (5%)
  matrix products  19.5 us (4%)
  between operations  15.3 us (3%)
    ppermute x16, waiting for transfers between devices, padded_2(): before = lax.ppermute(last, axis, up)  80.3 us
    ppermute x16, starting transfers between devices, padded_2(): before = lax.ppermute(last, axis, up)  78.1 us
    ppermute x16, waiting for transfers between devices, padded_2(): after = lax.ppermute(first, axis, down)  62.4 us
    all_gather x2, blocking collectives, on_device(): gathered = jnp.concatenate(lax.all_gather(speed_rounded, 'tcol'), axis=1)  61.5 us
    all_gather x1, blocking collectives, on_device(): lax.all_gather(wet_normal, 'tcol', axis=1, tiled=True)  31.1 us
    all_gather x1, blocking collectives, on_device(): lax.all_gather(wet_position, 'tcol', axis=1, tiled=True)  30.7 us
    ppermute x16, starting transfers between devices, padded_2(): after = lax.ppermute(first, axis, down)  20.6 us
    all_gather x1, blocking collectives, on_device(): lax.all_gather(wet_area, 'tcol', axis=0, tiled=True)  20.5 us
  transfers between devices with their start and end apart: 34, of which 29 were waited for; matrix products, arithmetic and copies ran while one was open for 9% of the time, Pallas kernels for 0%

profile of v1, /device:TPU:0, one launch (start us, length us, event | category | flops | bytes accessed | tf_op | source)
XLA Modules:
  0.0 488.0 jit_solution(6184426121161419390)
XLA Ops:
  8.1 4.9 %collective-permute-start.1 = (f32[3,3,8,256]{3,2,1,0:T(8,128)S(1)}, f32[3,3,8,256]{3,2,1,0:T(8,128)S(1)}, u32[]{:S(2)}, u32[]{:S(2)}) collective-permute-start(f32[3,3,8,256]{3,2,1,0:T(8,128)S(1)} %get-tuple-element.397), channel_id=1, source_target_pairs={{0,8},{8,16},{16,24},{1,9},{9,17},{17,25},{2,10},{10,18},{18,26},{... | collective-permute-start | bytes 221192 | tf_op jit(solution)/shard_map/ppermute | solution.py:25
  16.6 31.1 %all_gather.25 = f32[3,2048]{1,0:T(4,128)S(1)} all-gather(f32[3,256]{1,0:T(4,128)} %param.17), channel_id=1, replica_groups=mesh['group'=2,'trow'=2,'tcol'=8] {'tcol'}, dimensions={1}, use_global_device_ids=true | all-gather | bytes 27648 | tf_op jit(solution)/shard_map/all_gather | solution.py:119
  47.6 30.7 %all_gather.27 = f32[3,2048]{1,0:T(4,128)S(1)} all-gather(f32[3,256]{1,0:T(4,128)} %param.16), channel_id=1, replica_groups=mesh['group'=2,'trow'=2,'tcol'=8] {'tcol'}, dimensions={1}, use_global_device_ids=true | all-gather | bytes 27648 | tf_op jit(solution)/shard_map/all_gather | solution.py:118
  78.4 12.3 %all_gather.26 = f32[3,1024]{1,0:T(4,128)} all-gather(f32[3,256]{1,0:T(4,128)} %param.16), channel_id=1, replica_groups=mesh['group'=2,'trow'=2,'tcol'=8] {'group','trow'}, dimensions={1}, use_global_device_ids=true | all-gather | bytes 15360 | tf_op jit(solution)/shard_map/all_gather | solution.py:116
  94.1 30.7 %all-gather = bf16[512,256]{1,0:T(8,128)(2,1)S(1)} all-gather(bf16[64,256]{1,0:T(8,128)(2,1)S(1)} %copy.68), channel_id=2, replica_groups=mesh['group'=2,'trow'=2,'tcol'=8] {'tcol'}, dimensions={0}, use_global_device_ids=true | all-gather | bytes 294912 | tf_op jit(solution)/shard_map/all_gather | solution.py:130
  124.8 20.5 %all-gather.2 = f32[8,1,256]{2,1,0:T(1,128)S(1)} all-gather(f32[1,1,256]{2,1,0:T(1,128)S(1)} %bitcast.203), channel_id=1, replica_groups=mesh['group'=2,'trow'=2,'tcol'=8] {'tcol'}, dimensions={0}, use_global_device_ids=true | all-gather | bytes 9216 | tf_op jit(solution)/shard_map/all_gather | solution.py:120
  145.4 11.3 %while.26 = (s32[]{:T(128)}, f32[64,1024]{1,0:T(8,128)S(1)}, f32[2048]{0:T(1024)S(1)}, f32[3,2048]{1,0:T(4,128)S(1)}, f32[3,1024]{1,0:T(4,128)}, /*index=5*/f32[...) while((s32[]{:T(128)}, f32[64,1024]{1,0:T(8,128)S(1)}, ...), condition=%wide.region_1.3_spmd, body=%wide.region_0.0_spmd.sunk | while | flops 154140672 | bytes 567507 | solution.py:110
  161.6 5.4 %collective-permute-start.3 = (f32[3,38,3,256]{3,2,1,0:T(4,128)}, f32[3,38,3,256]{3,2,1,0:T(4,128)}, u32[]{:S(2)}, u32[]{:S(2)}) collective-permute-start(f32[3,38,3,256]{3,2,1,0:T(4,128)} %get-tuple-element.346), channel_id=1, source_target_pairs={{0,1},{1,2},{2,3},{3,4},{4,5},{5,6},{6,7},{8,9},{9,10},{10,11},{11... | collective-permute-start | bytes 1050632 | tf_op jit(solution)/shard_map/ppermute | solution.py:25
  172.5 5.7 %fusion.156 = f32[3,32,8,256]{3,2,1,0:T(8,128)S(1)} fusion(f32[3,38,8,256]{3,2,1,0:T(8,128)} %copy-done.5, f32[3,38,3,256]{3,2,1,0:T(4,128)} %collective-permute-done.3, f32[3,38,3,256]{3,2,1,0:T(4,128)} %copy-done.16, f32[3,35,8,256]{3,2,1,0:T(8,128)} %copy-done.3, f32[3,35,8,256]{3,2,1,0:T(8,128)S(1)} %get-tuple-element.401, ...), kind=kLoop, calls=%fused_computation.249 | loop fusion | flops 6094848 | bytes 9499648 | tf_op jit(solution)/shard_map/sub | solution.py:54
  189.7 5.2 %collective-permute-start.7 = (f32[3,38,3,256]{3,2,1,0:T(4,128)S(1)}, f32[3,38,3,256]{3,2,1,0:T(4,128)S(1)}, u32[]{:S(2)}, u32[]{:S(2)}) collective-permute-start(f32[3,38,3,256]{3,2,1,0:T(4,128)S(1)} %get-tuple-element.344), channel_id=1, source_target_pairs={{0,1},{1,2},{2,3},{3,4},{4,5},{5,6},{6,7},{8,9},{9,10},{10,11},{11... | collective-permute-start | bytes 1050632 | tf_op jit(solution)/shard_map/ppermute | solution.py:25
  195.4 8.8 %collective-permute-done.6 = f32[3,38,3,256]{3,2,1,0:T(4,128)S(1)} collective-permute-done((f32[3,38,3,256]{3,2,1,0:T(4,128)S(1)}, f32[3,38,3,256]{3,2,1,0:T(4,128)S(1)}, u32[]{:S(2)}, u32[]{:S(2)}) %collective-permute-start.6) | collective-permute-done | bytes 350240 | tf_op jit(solution)/shard_map/ppermute | solution.py:26
  204.2 10.2 %collective-permute-done.7 = f32[3,38,3,256]{3,2,1,0:T(4,128)S(1)} collective-permute-done((f32[3,38,3,256]{3,2,1,0:T(4,128)S(1)}, f32[3,38,3,256]{3,2,1,0:T(4,128)S(1)}, u32[]{:S(2)}, u32[]{:S(2)}) %collective-permute-start.7) | collective-permute-done | bytes 350240 | tf_op jit(solution)/shard_map/ppermute | solution.py:25
  226.5 5.0 %collective-permute-start.11 = (f32[3,38,3,256]{3,2,1,0:T(4,128)S(1)}, f32[3,38,3,256]{3,2,1,0:T(4,128)S(1)}, u32[]{:S(2)}, u32[]{:S(2)}) collective-permute-start(f32[3,38,3,256]{3,2,1,0:T(4,128)S(1)} %get-tuple-element.340), channel_id=1, source_target_pairs={{0,1},{1,2},{2,3},{3,4},{4,5},{5,6},{6,7},{8,9},{9,10},{10,11},{11... | collective-permute-start | bytes 1050632 | tf_op jit(solution)/shard_map/ppermute | solution.py:25
  232.0 8.6 %collective-permute-done.10 = f32[3,38,3,256]{3,2,1,0:T(4,128)S(1)} collective-permute-done((f32[3,38,3,256]{3,2,1,0:T(4,128)S(1)}, f32[3,38,3,256]{3,2,1,0:T(4,128)S(1)}, u32[]{:S(2)}, u32[]{:S(2)}) %collective-permute-start.10) | collective-permute-done | bytes 350240 | tf_op jit(solution)/shard_map/ppermute | solution.py:26
  240.6 10.2 %collective-permute-done.11 = f32[3,38,3,256]{3,2,1,0:T(4,128)S(1)} collective-permute-done((f32[3,38,3,256]{3,2,1,0:T(4,128)S(1)}, f32[3,38,3,256]{3,2,1,0:T(4,128)S(1)}, u32[]{:S(2)}, u32[]{:S(2)}) %collective-permute-start.11) | collective-permute-done | bytes 350240 | tf_op jit(solution)/shard_map/ppermute | solution.py:25
  263.1 5.0 %collective-permute-start.15 = (f32[3,38,3,256]{3,2,1,0:T(4,128)S(1)}, f32[3,38,3,256]{3,2,1,0:T(4,128)S(1)}, u32[]{:S(2)}, u32[]{:S(2)}) collective-permute-start(f32[3,38,3,256]{3,2,1,0:T(4,128)S(1)} %get-tuple-element.336), channel_id=1, source_target_pairs={{0,1},{1,2},{2,3},{3,4},{4,5},{5,6},{6,7},{8,9},{9,10},{10,11},{11... | collective-permute-start | bytes 1050632 | tf_op jit(solution)/shard_map/ppermute | solution.py:25
  268.6 9.1 %collective-permute-done.14 = f32[3,38,3,256]{3,2,1,0:T(4,128)S(1)} collective-permute-done((f32[3,38,3,256]{3,2,1,0:T(4,128)S(1)}, f32[3,38,3,256]{3,2,1,0:T(4,128)S(1)}, u32[]{:S(2)}, u32[]{:S(2)}) %collective-permute-start.14) | collective-permute-done | bytes 350240 | tf_op jit(solution)/shard_map/ppermute | solution.py:26
  277.7 10.2 %collective-permute-done.15 = f32[3,38,3,256]{3,2,1,0:T(4,128)S(1)} collective-permute-done((f32[3,38,3,256]{3,2,1,0:T(4,128)S(1)}, f32[3,38,3,256]{3,2,1,0:T(4,128)S(1)}, u32[]{:S(2)}, u32[]{:S(2)}) %collective-permute-start.15) | collective-permute-done | bytes 350240 | tf_op jit(solution)/shard_map/ppermute | solution.py:25
  293.5 30.8 %all-gather.1 = bf16[512,256]{1,0:T(8,128)(2,1)S(1)} all-gather(bf16[64,256]{1,0:T(8,128)(2,1)S(1)} %copy.75), channel_id=3, replica_groups=mesh['group'=2,'trow'=2,'tcol'=8] {'tcol'}, dimensions={0}, use_global_device_ids=true | all-gather | bytes 294912 | tf_op jit(solution)/shard_map/all_gather | solution.py:130
  330.4 11.3 %while.27 = (s32[]{:T(128)}, f32[64,1024]{1,0:T(8,128)S(1)}, f32[2048]{0:T(1024)S(1)}, f32[3,2048]{1,0:T(4,128)S(1)}, f32[3,1024]{1,0:T(4,128)}, /*index=5*/f32[...) while((s32[]{:T(128)}, f32[64,1024]{1,0:T(8,128)S(1)}, ...), condition=%wide.region_4.6_spmd, body=%wide.region_3.5_spmd.sunk | while | flops 154140672 | bytes 567507 | solution.py:110
  344.0 5.3 %collective-permute-start.19 = (f32[3,38,3,256]{3,2,1,0:T(4,128)S(1)}, f32[3,38,3,256]{3,2,1,0:T(4,128)}, u32[]{:S(2)}, u32[]{:S(2)}) collective-permute-start(f32[3,38,3,256]{3,2,1,0:T(4,128)S(1)} %get-tuple-element.332), channel_id=1, source_target_pairs={{0,1},{1,2},{2,3},{3,4},{4,5},{5,6},{6,7},{8,9},{9,10},{10,11},{11... | collective-permute-start | bytes 1050632 | tf_op jit(solution)/shard_map/ppermute | solution.py:25
  350.8 5.0 %collective-permute-done.18 = f32[3,38,3,256]{3,2,1,0:T(4,128)} collective-permute-done((f32[3,38,3,256]{3,2,1,0:T(4,128)}, f32[3,38,3,256]{3,2,1,0:T(4,128)}, u32[]{:S(2)}, u32[]{:S(2)}) %collective-permute-start.18) | collective-permute-done | bytes 350240 | tf_op jit(solution)/shard_map/ppermute | solution.py:26
  355.9 8.2 %collective-permute-done.19 = f32[3,38,3,256]{3,2,1,0:T(4,128)} collective-permute-done((f32[3,38,3,256]{3,2,1,0:T(4,128)S(1)}, f32[3,38,3,256]{3,2,1,0:T(4,128)}, u32[]{:S(2)}, u32[]{:S(2)}) %collective-permute-start.19) | collective-permute-done | bytes 350240 | tf_op jit(solution)/shard_map/ppermute | solution.py:25
  380.0 4.9 collective-permute-start.23
  385.3 8.6 %collective-permute-done.22 = f32[3,38,3,256]{3,2,1,0:T(4,128)S(1)} collective-permute-done((f32[3,38,3,256]{3,2,1,0:T(4,128)S(1)}, f32[3,38,3,256]{3,2,1,0:T(4,128)S(1)}, u32[]{:S(2)}, u32[]{:S(2)}) %collective-permute-start.22) | collective-permute-done | bytes 350240 | tf_op jit(solution)/shard_map/ppermute | solution.py:26
  394.0 10.2 %collective-permute-done.23 = f32[3,38,3,256]{3,2,1,0:T(4,128)S(1)} collective-permute-done((f32[3,38,3,256]{3,2,1,0:T(4,128)S(1)}, f32[3,38,3,256]{3,2,1,0:T(4,128)S(1)}, u32[]{:S(2)}, u32[]{:S(2)}) %collective-permute-start.23) | collective-permute-done | bytes 350240 | tf_op jit(solution)/shard_map/ppermute | solution.py:25
  416.2 5.3 %collective-permute-start.27 = (f32[3,38,3,256]{3,2,1,0:T(4,128)S(1)}, f32[3,38,3,256]{3,2,1,0:T(4,128)S(1)}, u32[]{:S(2)}, u32[]{:S(2)}) collective-permute-start(f32[3,38,3,256]{3,2,1,0:T(4,128)S(1)} %get-tuple-element.324), channel_id=1, source_target_pairs={{0,1},{1,2},{2,3},{3,4},{4,5},{5,6},{6,7},{8,9},{9,10},{10,11},{11... | collective-permute-start | bytes 1050632 | tf_op jit(solution)/shard_map/ppermute | solution.py:25
  422.0 8.9 %collective-permute-done.26 = f32[3,38,3,256]{3,2,1,0:T(4,128)S(1)} collective-permute-done((f32[3,38,3,256]{3,2,1,0:T(4,128)S(1)}, f32[3,38,3,256]{3,2,1,0:T(4,128)S(1)}, u32[]{:S(2)}, u32[]{:S(2)}) %collective-permute-start.26) | collective-permute-done | bytes 350240 | tf_op jit(solution)/shard_map/ppermute | solution.py:26
  430.8 10.2 %collective-permute-done.27 = f32[3,38,3,256]{3,2,1,0:T(4,128)S(1)} collective-permute-done((f32[3,38,3,256]{3,2,1,0:T(4,128)S(1)}, f32[3,38,3,256]{3,2,1,0:T(4,128)S(1)}, u32[]{:S(2)}, u32[]{:S(2)}) %collective-permute-start.27) | collective-permute-done | bytes 350240 | tf_op jit(solution)/shard_map/ppermute | solution.py:25
  453.0 5.0 %collective-permute-start.31 = (f32[3,38,3,256]{3,2,1,0:T(4,128)S(1)}, f32[3,38,3,256]{3,2,1,0:T(4,128)S(1)}, u32[]{:S(2)}, u32[]{:S(2)}) collective-permute-start(f32[3,38,3,256]{3,2,1,0:T(4,128)S(1)} %get-tuple-element.320), channel_id=1, source_target_pairs={{0,1},{1,2},{2,3},{3,4},{4,5},{5,6},{6,7},{8,9},{9,10},{10,11},{11... | collective-permute-start | bytes 1050632 | tf_op jit(solution)/shard_map/ppermute | solution.py:25
  458.5 8.6 %collective-permute-done.30 = f32[3,38,3,256]{3,2,1,0:T(4,128)S(1)} collective-permute-done((f32[3,38,3,256]{3,2,1,0:T(4,128)S(1)}, f32[3,38,3,256]{3,2,1,0:T(4,128)S(1)}, u32[]{:S(2)}, u32[]{:S(2)}) %collective-permute-start.30) | collective-permute-done | bytes 350240 | tf_op jit(solution)/shard_map/ppermute | solution.py:26
  467.1 10.2 %collective-permute-done.31 = f32[3,38,3,256]{3,2,1,0:T(4,128)S(1)} collective-permute-done((f32[3,38,3,256]{3,2,1,0:T(4,128)S(1)}, f32[3,38,3,256]{3,2,1,0:T(4,128)S(1)}, u32[]{:S(2)}, u32[]{:S(2)}) %collective-permute-start.31) | collective-permute-done | bytes 350240 | tf_op jit(solution)/shard_map/ppermute | solution.py:25
  (231 shorter events, 137.7 us)
Async XLA Ops:
  7.2 171.1 %reduce-scatter.3.cloned.1.call-start = ((), (), s32[]{:S(2)}) async-start(), calls=%async_computation.2 | async-start | bytes 655360 | tf_op jit(solution)/shard_map/reduce_scatter | solution.py:132
  8.1 149.7 %collective-permute-start.1 = (f32[3,3,8,256]{3,2,1,0:T(8,128)S(1)}, f32[3,3,8,256]{3,2,1,0:T(8,128)S(1)}, u32[]{:S(2)}, u32[]{:S(2)}) collective-permute-start(f32[3,3,8,256]{3,2,1,0:T(8,128)S(1)} %get-tuple-element.397), channel_id=1, source_target_pairs={{0,8},{8,16},{16,24},{1,9},{9,17},{17,25},{2,10},{10,18},{18,26},{... | collective-permute-start | bytes 221192 | tf_op jit(solution)/shard_map/ppermute | solution.py:25
  13.1 145.1 %collective-permute-start = (f32[3,3,8,256]{3,2,1,0:T(8,128)S(1)}, f32[3,3,8,256]{3,2,1,0:T(8,128)S(1)}, u32[]{:S(2)}, u32[]{:S(2)}) collective-permute-start(f32[3,3,8,256]{3,2,1,0:T(8,128)S(1)} %get-tuple-element.396), channel_id=1, source_target_pairs={{8,0},{16,8},{24,16},{9,1},{17,9},{25,17},{10,2},{18,10},{26,18},{... | collective-permute-start | bytes 221192 | tf_op jit(solution)/shard_map/ppermute | solution.py:26
  157.8 210.9 %reduce-scatter.5.cloned.1.call-start = ((), (), s32[]{:S(2)}) async-start(), calls=%async_computation.3 | async-start | bytes 655360 | tf_op jit(solution)/shard_map/reduce_scatter | solution.py:132
  160.3 10.7 %collective-permute-start.2 = (f32[3,38,3,256]{3,2,1,0:T(4,128)}, f32[3,38,3,256]{3,2,1,0:T(4,128)S(1)}, u32[]{:S(2)}, u32[]{:S(2)}) collective-permute-start(f32[3,38,3,256]{3,2,1,0:T(4,128)} %get-tuple-element.345), channel_id=1, source_target_pairs={{1,0},{2,1},{3,2},{4,3},{5,4},{6,5},{7,6},{9,8},{10,9},{11,10},{12... | collective-permute-start | bytes 1050632 | tf_op jit(solution)/shard_map/ppermute | solution.py:26
  161.6 10.9 %collective-permute-start.3 = (f32[3,38,3,256]{3,2,1,0:T(4,128)}, f32[3,38,3,256]{3,2,1,0:T(4,128)}, u32[]{:S(2)}, u32[]{:S(2)}) collective-permute-start(f32[3,38,3,256]{3,2,1,0:T(4,128)} %get-tuple-element.346), channel_id=1, source_target_pairs={{0,1},{1,2},{2,3},{3,4},{4,5},{5,6},{6,7},{8,9},{9,10},{10,11},{11... | collective-permute-start | bytes 1050632 | tf_op jit(solution)/shard_map/ppermute | solution.py:25
  180.3 6.2 %collective-permute-start.4 = (f32[3,3,8,256]{3,2,1,0:T(8,128)S(1)}, f32[3,3,8,256]{3,2,1,0:T(8,128)S(1)}, u32[]{:S(2)}, u32[]{:S(2)}) collective-permute-start(f32[3,3,8,256]{3,2,1,0:T(8,128)S(1)} %get-tuple-element.387), channel_id=1, source_target_pairs={{8,0},{16,8},{24,16},{9,1},{17,9},{25,17},{10,2},{18,10},{26,18},{... | collective-permute-start | bytes 221192 | tf_op jit(solution)/shard_map/ppermute | solution.py:26
  181.6 6.5 %collective-permute-start.5 = (f32[3,3,8,256]{3,2,1,0:T(8,128)S(1)}, f32[3,3,8,256]{3,2,1,0:T(8,128)S(1)}, u32[]{:S(2)}, u32[]{:S(2)}) collective-permute-start(f32[3,3,8,256]{3,2,1,0:T(8,128)S(1)} %get-tuple-element.388), channel_id=1, source_target_pairs={{0,8},{8,16},{16,24},{1,9},{9,17},{17,25},{2,10},{10,18},{18,26},{... | collective-permute-start | bytes 221192 | tf_op jit(solution)/shard_map/ppermute | solution.py:25
  188.4 15.8 %collective-permute-start.6 = (f32[3,38,3,256]{3,2,1,0:T(4,128)S(1)}, f32[3,38,3,256]{3,2,1,0:T(4,128)S(1)}, u32[]{:S(2)}, u32[]{:S(2)}) collective-permute-start(f32[3,38,3,256]{3,2,1,0:T(4,128)S(1)} %get-tuple-element.343), channel_id=1, source_target_pairs={{1,0},{2,1},{3,2},{4,3},{5,4},{6,5},{7,6},{9,8},{10,9},{11,10},{12... | collective-permute-start | bytes 1050632 | tf_op jit(solution)/shard_map/ppermute | solution.py:26
  189.7 24.7 %collective-permute-start.7 = (f32[3,38,3,256]{3,2,1,0:T(4,128)S(1)}, f32[3,38,3,256]{3,2,1,0:T(4,128)S(1)}, u32[]{:S(2)}, u32[]{:S(2)}) collective-permute-start(f32[3,38,3,256]{3,2,1,0:T(4,128)S(1)} %get-tuple-element.344), channel_id=1, source_target_pairs={{0,1},{1,2},{2,3},{3,4},{4,5},{5,6},{6,7},{8,9},{9,10},{10,11},{11... | collective-permute-start | bytes 1050632 | tf_op jit(solution)/shard_map/ppermute | solution.py:25
  217.2 6.2 %collective-permute-start.8 = (f32[3,3,8,256]{3,2,1,0:T(8,128)S(1)}, f32[3,3,8,256]{3,2,1,0:T(8,128)S(1)}, u32[]{:S(2)}, u32[]{:S(2)}) collective-permute-start(f32[3,3,8,256]{3,2,1,0:T(8,128)S(1)} %get-tuple-element.381), channel_id=1, source_target_pairs={{8,0},{16,8},{24,16},{9,1},{17,9},{25,17},{10,2},{18,10},{26,18},{... | collective-permute-start | bytes 221192 | tf_op jit(solution)/shard_map/ppermute | solution.py:26
  218.5 6.5 %collective-permute-start.9 = (f32[3,3,8,256]{3,2,1,0:T(8,128)S(1)}, f32[3,3,8,256]{3,2,1,0:T(8,128)S(1)}, u32[]{:S(2)}, u32[]{:S(2)}) collective-permute-start(f32[3,3,8,256]{3,2,1,0:T(8,128)S(1)} %get-tuple-element.382), channel_id=1, source_target_pairs={{0,8},{8,16},{16,24},{1,9},{9,17},{17,25},{2,10},{10,18},{18,26},{... | collective-permute-start | bytes 221192 | tf_op jit(solution)/shard_map/ppermute | solution.py:25
  225.2 15.4 %collective-permute-start.10 = (f32[3,38,3,256]{3,2,1,0:T(4,128)S(1)}, f32[3,38,3,256]{3,2,1,0:T(4,128)S(1)}, u32[]{:S(2)}, u32[]{:S(2)}) collective-permute-start(f32[3,38,3,256]{3,2,1,0:T(4,128)S(1)} %get-tuple-element.339), channel_id=1, source_target_pairs={{1,0},{2,1},{3,2},{4,3},{5,4},{6,5},{7,6},{9,8},{10,9},{11,10},{12... | collective-permute-start | bytes 1050632 | tf_op jit(solution)/shard_map/ppermute | solution.py:26
  226.5 24.3 %collective-permute-start.11 = (f32[3,38,3,256]{3,2,1,0:T(4,128)S(1)}, f32[3,38,3,256]{3,2,1,0:T(4,128)S(1)}, u32[]{:S(2)}, u32[]{:S(2)}) collective-permute-start(f32[3,38,3,256]{3,2,1,0:T(4,128)S(1)} %get-tuple-element.340), channel_id=1, source_target_pairs={{0,1},{1,2},{2,3},{3,4},{4,5},{5,6},{6,7},{8,9},{9,10},{10,11},{11... | collective-permute-start | bytes 1050632 | tf_op jit(solution)/shard_map/ppermute | solution.py:25
  253.3 6.2 %collective-permute-start.12 = (f32[3,3,8,256]{3,2,1,0:T(8,128)S(1)}, f32[3,3,8,256]{3,2,1,0:T(8,128)S(1)}, u32[]{:S(2)}, u32[]{:S(2)}) collective-permute-start(f32[3,3,8,256]{3,2,1,0:T(8,128)S(1)} %get-tuple-element.375), channel_id=1, source_target_pairs={{8,0},{16,8},{24,16},{9,1},{17,9},{25,17},{10,2},{18,10},{26,18},{... | collective-permute-start | bytes 221192 | tf_op jit(solution)/shard_map/ppermute | solution.py:26
  254.6 6.5 %collective-permute-start.13 = (f32[3,3,8,256]{3,2,1,0:T(8,128)S(1)}, f32[3,3,8,256]{3,2,1,0:T(8,128)S(1)}, u32[]{:S(2)}, u32[]{:S(2)}) collective-permute-start(f32[3,3,8,256]{3,2,1,0:T(8,128)S(1)} %get-tuple-element.376), channel_id=1, source_target_pairs={{0,8},{8,16},{16,24},{1,9},{9,17},{17,25},{2,10},{10,18},{18,26},{... | collective-permute-start | bytes 221192 | tf_op jit(solution)/shard_map/ppermute | solution.py:25
  261.8 15.9 %collective-permute-start.14 = (f32[3,38,3,256]{3,2,1,0:T(4,128)S(1)}, f32[3,38,3,256]{3,2,1,0:T(4,128)S(1)}, u32[]{:S(2)}, u32[]{:S(2)}) collective-permute-start(f32[3,38,3,256]{3,2,1,0:T(4,128)S(1)} %get-tuple-element.335), channel_id=1, source_target_pairs={{1,0},{2,1},{3,2},{4,3},{5,4},{6,5},{7,6},{9,8},{10,9},{11,10},{12... | collective-permute-start | bytes 1050632 | tf_op jit(solution)/shard_map/ppermute | solution.py:26
  263.1 24.8 %collective-permute-start.15 = (f32[3,38,3,256]{3,2,1,0:T(4,128)S(1)}, f32[3,38,3,256]{3,2,1,0:T(4,128)S(1)}, u32[]{:S(2)}, u32[]{:S(2)}) collective-permute-start(f32[3,38,3,256]{3,2,1,0:T(4,128)S(1)} %get-tuple-element.336), channel_id=1, source_target_pairs={{0,1},{1,2},{2,3},{3,4},{4,5},{5,6},{6,7},{8,9},{9,10},{10,11},{11... | collective-permute-start | bytes 1050632 | tf_op jit(solution)/shard_map/ppermute | solution.py:25
  324.2 17.5 %collective-permute-start.16 = (f32[3,3,8,256]{3,2,1,0:T(8,128)S(1)}, f32[3,3,8,256]{3,2,1,0:T(8,128)S(1)}, u32[]{:S(2)}, u32[]{:S(2)}) collective-permute-start(f32[3,3,8,256]{3,2,1,0:T(8,128)S(1)} %get-tuple-element.369), channel_id=1, source_target_pairs={{8,0},{16,8},{24,16},{9,1},{17,9},{25,17},{10,2},{18,10},{26,18},{... | collective-permute-start | bytes 221192 | tf_op jit(solution)/shard_map/ppermute | solution.py:26
  325.5 16.2 %collective-permute-start.17 = (f32[3,3,8,256]{3,2,1,0:T(8,128)S(1)}, f32[3,3,8,256]{3,2,1,0:T(8,128)S(1)}, u32[]{:S(2)}, u32[]{:S(2)}) collective-permute-start(f32[3,3,8,256]{3,2,1,0:T(8,128)S(1)} %get-tuple-element.370), channel_id=1, source_target_pairs={{0,8},{8,16},{16,24},{1,9},{9,17},{17,25},{2,10},{10,18},{18,26},{... | collective-permute-start | bytes 221192 | tf_op jit(solution)/shard_map/ppermute | solution.py:25
  342.7 13.1 %collective-permute-start.18 = (f32[3,38,3,256]{3,2,1,0:T(4,128)}, f32[3,38,3,256]{3,2,1,0:T(4,128)}, u32[]{:S(2)}, u32[]{:S(2)}) collective-permute-start(f32[3,38,3,256]{3,2,1,0:T(4,128)} %get-tuple-element.331), channel_id=1, source_target_pairs={{1,0},{2,1},{3,2},{4,3},{5,4},{6,5},{7,6},{9,8},{10,9},{11,10},{12... | collective-permute-start | bytes 1050632 | tf_op jit(solution)/shard_map/ppermute | solution.py:26
  344.0 20.0 %collective-permute-start.19 = (f32[3,38,3,256]{3,2,1,0:T(4,128)S(1)}, f32[3,38,3,256]{3,2,1,0:T(4,128)}, u32[]{:S(2)}, u32[]{:S(2)}) collective-permute-start(f32[3,38,3,256]{3,2,1,0:T(4,128)S(1)} %get-tuple-element.332), channel_id=1, source_target_pairs={{0,1},{1,2},{2,3},{3,4},{4,5},{5,6},{6,7},{8,9},{9,10},{10,11},{11... | collective-permute-start | bytes 1050632 | tf_op jit(solution)/shard_map/ppermute | solution.py:25
  370.7 6.2 %collective-permute-start.20 = (f32[3,3,8,256]{3,2,1,0:T(8,128)S(1)}, f32[3,3,8,256]{3,2,1,0:T(8,128)S(1)}, u32[]{:S(2)}, u32[]{:S(2)}) collective-permute-start(f32[3,3,8,256]{3,2,1,0:T(8,128)S(1)} %get-tuple-element.363), channel_id=1, source_target_pairs={{8,0},{16,8},{24,16},{9,1},{17,9},{25,17},{10,2},{18,10},{26,18},{... | collective-permute-start | bytes 221192 | tf_op jit(solution)/shard_map/ppermute | solution.py:26
  372.0 6.5 %collective-permute-start.21 = (f32[3,3,8,256]{3,2,1,0:T(8,128)S(1)}, f32[3,3,8,256]{3,2,1,0:T(8,128)S(1)}, u32[]{:S(2)}, u32[]{:S(2)}) collective-permute-start(f32[3,3,8,256]{3,2,1,0:T(8,128)S(1)} %get-tuple-element.364), channel_id=1, source_target_pairs={{0,8},{8,16},{16,24},{1,9},{9,17},{17,25},{2,10},{10,18},{18,26},{... | collective-permute-start | bytes 221192 | tf_op jit(solution)/shard_map/ppermute | solution.py:25
  378.7 15.2 %collective-permute-start.22 = (f32[3,38,3,256]{3,2,1,0:T(4,128)S(1)}, f32[3,38,3,256]{3,2,1,0:T(4,128)S(1)}, u32[]{:S(2)}, u32[]{:S(2)}) collective-permute-start(f32[3,38,3,256]{3,2,1,0:T(4,128)S(1)} %get-tuple-element.327), channel_id=1, source_target_pairs={{1,0},{2,1},{3,2},{4,3},{5,4},{6,5},{7,6},{9,8},{10,9},{11,10},{12... | collective-permute-start | bytes 1050632 | tf_op jit(solution)/shard_map/ppermute | solution.py:26
  380.0 24.1 %collective-permute-start.23 = (f32[3,38,3,256]{3,2,1,0:T(4,128)S(1)}, f32[3,38,3,256]{3,2,1,0:T(4,128)S(1)}, u32[]{:S(2)}, u32[]{:S(2)}) collective-permute-start(f32[3,38,3,256]{3,2,1,0:T(4,128)S(1)} %get-tuple-element.328), channel_id=1, source_target_pairs={{0,1},{1,2},{2,3},{3,4},{4,5},{5,6},{6,7},{8,9},{9,10},{10,11},{11... | collective-permute-start | bytes 1050632 | tf_op jit(solution)/shard_map/ppermute | solution.py:25
  408.2 6.5 %collective-permute-start.25 = (f32[3,3,8,256]{3,2,1,0:T(8,128)S(1)}, f32[3,3,8,256]{3,2,1,0:T(8,128)S(1)}, u32[]{:S(2)}, u32[]{:S(2)}) collective-permute-start(f32[3,3,8,256]{3,2,1,0:T(8,128)S(1)} %get-tuple-element.358), channel_id=1, source_target_pairs={{0,8},{8,16},{16,24},{1,9},{9,17},{17,25},{2,10},{10,18},{18,26},{... | collective-permute-start | bytes 221192 | tf_op jit(solution)/shard_map/ppermute | solution.py:25
  414.9 15.9 %collective-permute-start.26 = (f32[3,38,3,256]{3,2,1,0:T(4,128)S(1)}, f32[3,38,3,256]{3,2,1,0:T(4,128)S(1)}, u32[]{:S(2)}, u32[]{:S(2)}) collective-permute-start(f32[3,38,3,256]{3,2,1,0:T(4,128)S(1)} %get-tuple-element.323), channel_id=1, source_target_pairs={{1,0},{2,1},{3,2},{4,3},{5,4},{6,5},{7,6},{9,8},{10,9},{11,10},{12... | collective-permute-start | bytes 1050632 | tf_op jit(solution)/shard_map/ppermute | solution.py:26
  416.2 24.8 %collective-permute-start.27 = (f32[3,38,3,256]{3,2,1,0:T(4,128)S(1)}, f32[3,38,3,256]{3,2,1,0:T(4,128)S(1)}, u32[]{:S(2)}, u32[]{:S(2)}) collective-permute-start(f32[3,38,3,256]{3,2,1,0:T(4,128)S(1)} %get-tuple-element.324), channel_id=1, source_target_pairs={{0,1},{1,2},{2,3},{3,4},{4,5},{5,6},{6,7},{8,9},{9,10},{10,11},{11... | collective-permute-start | bytes 1050632 | tf_op jit(solution)/shard_map/ppermute | solution.py:25
  444.9 6.5 %collective-permute-start.29 = (f32[3,3,8,256]{3,2,1,0:T(8,128)S(1)}, f32[3,3,8,256]{3,2,1,0:T(8,128)S(1)}, u32[]{:S(2)}, u32[]{:S(2)}) collective-permute-start(f32[3,3,8,256]{3,2,1,0:T(8,128)S(1)} %get-tuple-element.352), channel_id=1, source_target_pairs={{0,8},{8,16},{16,24},{1,9},{9,17},{17,25},{2,10},{10,18},{18,26},{... | collective-permute-start | bytes 221192 | tf_op jit(solution)/shard_map/ppermute | solution.py:25
  451.7 15.4 %collective-permute-start.30 = (f32[3,38,3,256]{3,2,1,0:T(4,128)S(1)}, f32[3,38,3,256]{3,2,1,0:T(4,128)S(1)}, u32[]{:S(2)}, u32[]{:S(2)}) collective-permute-start(f32[3,38,3,256]{3,2,1,0:T(4,128)S(1)} %get-tuple-element.319), channel_id=1, source_target_pairs={{1,0},{2,1},{3,2},{4,3},{5,4},{6,5},{7,6},{9,8},{10,9},{11,10},{12... | collective-permute-start | bytes 1050632 | tf_op jit(solution)/shard_map/ppermute | solution.py:26
  453.0 24.3 %collective-permute-start.31 = (f32[3,38,3,256]{3,2,1,0:T(4,128)S(1)}, f32[3,38,3,256]{3,2,1,0:T(4,128)S(1)}, u32[]{:S(2)}, u32[]{:S(2)}) collective-permute-start(f32[3,38,3,256]{3,2,1,0:T(4,128)S(1)} %get-tuple-element.320), channel_id=1, source_target_pairs={{0,1},{1,2},{2,3},{3,4},{4,5},{5,6},{6,7},{8,9},{9,10},{10,11},{11... | collective-permute-start | bytes 1050632 | tf_op jit(solution)/shard_map/ppermute | solution.py:25
  (36 other events, 634.4 us)
Sparse Core Ops, SparseCore 0:
  157.9 18.1 reduce-scatter.2
  350.7 17.9 reduce-scatter.4
